TPU v7x, 256 devices: a whole 4x4x8 slice. The times are simulated.
256 devices in a mesh: bins: 64 (over z, y, x_hi), det: 4 (over x_lo, core).
Axes of the slice: x: 4 (x_hi: 2, x_lo: 2; x = x_hi * 2 + x_lo), y: 4, z: 8, core: 2. Of those that a mesh axis runs over, the one named last changes fastest.
Arguments:
- strain: float32 [4, 17408], P('det', 'bins'), may hold values from -6 to 6
- filters: bfloat16 [64, 512, 1024], P('bins'), may hold values from -0.1875 to 0.1875
- mixing: bfloat16 [64, 2, 256, 512], P('bins'), may hold values from -0.375 to 0.375
- counts: int32 [64], P('bins'), may hold values from 64 to 512
- rate_bands: int32 [64], P('bins'), may hold values from 0 to 4
Outputs:
- network_power: float32 [64, 256, 512], P('bins', 'det')
All inputs are finite; a program needn't handle non-finite values.
Results may differ from a plain program's by a relative error of at most 0.0032.
Values may be sent and summed in bfloat16 or wider, within the bound.
A program may use at most 64 MiB of HBM per device.

v0:
```python
import jax
import jax.numpy as jnp
from jax import lax
from jax.experimental import pallas as pl
from jax.experimental.pallas import tpu as pltpu
from jax.sharding import PartitionSpec as P

DETS = 4
KMAX = 512
TAPS = 1024
TPL = 256
OUT0 = 512
SAMPLES = 17408
SHARD = 272
NZ, NY, NX = 8, 4, 2
NE = NX * DETS
PART = TPL // DETS
LANES = 128
MESH = pl.DeviceIdType.MESH
F32 = jnp.float32
BF16 = jnp.bfloat16
WIDTH = (272, 136, 68, 34, 17)
COLUMN = (0, 0, 136, 204, 238)
START = tuple((SAMPLES >> r) - (OUT0 >> r) - (TAPS - 1) for r in range(5))


def iota(shape, dim):
    return lax.broadcasted_iota(jnp.int32, shape, dim)


def ladder_matrix():
    col = iota((1, 2 * LANES), 1)
    sample = iota((3 * LANES, 2 * LANES), 0)
    matrix = jnp.zeros((3 * LANES, 2 * LANES), F32)
    for r in range(1, 5):
        here = (col >= COLUMN[r]) & (col < COLUMN[r] + WIDTH[r])
        matrix = jnp.where(here & ((sample >> r) == col - COLUMN[r]), 0.5**r, matrix)
    return matrix.astype(BF16)


def gather_kernel(
    counts_ref,
    strain_ref,
    filters_ref,
    mixing_ref,
    seen_ref,
    bank_ref,
    padded,
    column,
    filters,
    mixing,
    local_sem,
    zs,
    zr,
    ys,
    yr,
    es,
    er,
):
    at_bin = lax.axis_index("bins")
    det = lax.axis_index("det")
    z = at_bin // (NY * NX)
    y = (at_bin // NX) % NY
    xh = at_bin % NX
    e = xh * DETS + det

    def bin_of(z, y, xh):
        return (z * NY + y) * NX + xh

    z_peers = [(bin_of((z + k) % NZ, y, xh), det) for k in range(1, NZ)]
    y_peers = [(bin_of(z, (y + k) % NY, xh), det) for k in range(1, NY)]
    e_peers = []
    for k in range(1, NE):
        other = (e + k) % NE
        e_peers.append((bin_of(z, y, other // DETS), other % DETS))

    barrier = pltpu.get_barrier_semaphore()
    for peer in z_peers + y_peers + e_peers:
        pl.semaphore_signal(barrier, inc=1, device_id=peer, device_id_type=MESH)

    load_filters = pltpu.make_async_copy(filters_ref, filters, local_sem.at[0])
    load_filters.start()
    rows = pl.ds(pl.multiple_of(det * PART, PART), PART)
    load_mixing = pltpu.make_async_copy(mixing_ref.at[:, :, rows, :], mixing, local_sem.at[1])
    load_mixing.start()

    padded[...] = jnp.zeros_like(padded)
    padded[:, 0:SHARD] = strain_ref[...]
    samples = padded[...]
    high = samples.astype(BF16).astype(F32)
    middle = (samples - high).astype(BF16).astype(F32)
    low = samples - high - middle
    part = iota((8, 3 * LANES), 0)
    wide = [jnp.broadcast_to(p, (8, 3 * LANES)) for p in (high, middle, low)]
    parts = jnp.where(
        part == 0, wide[0], jnp.where(part == 1, wide[1], jnp.where(part == 2, wide[2], 0.0))
    )
    split = jnp.dot(parts.astype(BF16), ladder_matrix(), preferred_element_type=F32)
    ladder = jnp.sum(split, axis=0, keepdims=True)
    row = iota((8, LANES), 0)
    tile = jnp.zeros((8, LANES), F32)
    lines = [ladder[:, :LANES], ladder[:, LANES:]]
    lines += [samples[:, k * LANES : (k + 1) * LANES] for k in range(3)]
    for k, line in enumerate(lines):
        tile = jnp.where(row == k, jnp.broadcast_to(line, (8, LANES)), tile)
    own = pl.ds(pl.multiple_of(z * 8, 8), 8)
    column[own, :] = tile

    pl.semaphore_wait(barrier, NZ + NY + NE - 3)

    def send(ref, send_sem, recv_sem, peer):
        copy = pltpu.make_async_remote_copy(
            src_ref=ref,
            dst_ref=ref,
            send_sem=send_sem,
            recv_sem=recv_sem,
            device_id=peer,
            device_id_type=MESH,
        )
        copy.start()
        return copy

    z_copies = [send(column.at[own, :], zs.at[k], zr.at[k], p) for k, p in enumerate(z_peers)]

    load_mixing.wait()
    live = iota((1, KMAX), 1) < counts_ref[0]
    load_filters.wait()
    mixed = mixing[...].reshape(2 * PART, KMAX)
    mixed = jnp.where(live, mixed, jnp.zeros_like(mixed))
    bank = jnp.dot(mixed, filters[0], preferred_element_type=F32)
    bank = bank.astype(BF16)
    square = (LANES, LANES)
    turn = (iota(square, 0) + iota(square, 1) == LANES - 1).astype(F32).astype(BF16)
    for a in range(TAPS // LANES):
        taps = slice(a * LANES, (a + 1) * LANES)
        bank_ref[:, taps] = jnp.dot(bank[:, taps], turn, preferred_element_type=F32).astype(BF16)

    for copy in z_copies:
        copy.wait_recv()
    low_rows = column[pl.ds(1, 8, stride=8), :]
    last = column[8 * (NZ - 1) : 8 * NZ, :]
    before = column[8 * (NZ - 2) : 8 * (NZ - 1), :]
    high_rows = jnp.where(row == 5, jnp.broadcast_to(before[0:1], (8, LANES)), last)
    seen_ref[e, y] = jnp.concatenate([low_rows, high_rows], axis=0).astype(BF16)

    y_copies = [send(seen_ref.at[e, y], ys.at[k], yr.at[k], p) for k, p in enumerate(y_peers)]
    for copy in y_copies:
        copy.wait_recv()
    e_copies = [send(seen_ref.at[e], es.at[k], er.at[k], p) for k, p in enumerate(e_peers)]
    for copy in e_copies:
        copy.wait_recv()
    for copy in z_copies + y_copies + e_copies:
        copy.wait_send()


def flatten(r, seen_ref, flat):
    lane = iota((8, LANES), 1)
    row = iota((8, LANES), 0)
    halves = {4: "low", 3: "low", 2: "low", 1: "both", 0: "high"}[r]
    width = WIDTH[r]
    picks = []
    moved = [[] for _ in range(DETS)]
    out_row16 = iota((16, 8), 0)
    for y in range(NY):
        for xh in range(NX):
            j = y * NX + xh
            jobs = []
            if halves == "low":
                first = COLUMN[r] - LANES
                jobs.append((0, [8 * z + j for z in range(8)], 0, first, [width] * 8))
            if halves == "both":
                jobs.append((0, [8 * z + j for z in range(8)], LANES, 0, [8] * 8))
                jobs.append(
                    (1, [8 * 7 + j, 0, 0, 0, 0, 8 * 6 + j, 0, 0], 0, 0, [LANES, 0, 0, 0, 0, LANES, 0, 0])
                )
            if halves == "high":
                jobs.append((1, [8 * 7 + j] * 8, None, 0, [0, 0, LANES, LANES, 16, 0, 0, 0]))
            for half, shards, skip, first, widths in jobs:
                begin, shift = [], []
                for k in range(8):
                    extra = (k - 2) * LANES if skip is None else skip
                    at = width * shards[k] + extra - START[r]
                    begin.append(at)
                    shift.append((at - first) % LANES)
                stride = (shift[1] - shift[0]) % LANES
                if any((shift[k] - shift[0] - k * stride) % LANES for k in range(8)):
                    stride = None
                begin_row = jnp.zeros((8, LANES), jnp.int32)
                begin_col = jnp.zeros((16, 8), jnp.int32)
                wide = jnp.zeros((8, LANES), jnp.int32)
                for k in range(8):
                    begin_row = jnp.where(row == k, begin[k], begin_row)
                    begin_col = jnp.where(iota((16, 8), 1) == k, begin[k], begin_col)
                    wide = jnp.where(row == k, widths[k], wide)
                offset = (lane - begin_row) & (LANES - 1)
                wraps = ((begin_row & (LANES - 1)) + offset) >= LANES
                for wrap in (False, True):
                    picks.append((begin_col >> 7) + int(wrap) == out_row16)
                for d in range(DETS):
                    block = seen_ref[xh * DETS + d, y].astype(F32)[8 * half : 8 * half + 8]
                    if stride is None:
                        turned = jnp.zeros((8, LANES), F32)
                        for amount in sorted(set(s for s, w in zip(shift, widths) if w)):
                            rolled = pltpu.roll(block, amount, 1)
                            mask = jnp.zeros((8, LANES), jnp.bool_)
                            for k in range(8):
                                if shift[k] == amount:
                                    mask = mask | (row == k)
                            turned = jnp.where(mask, rolled, turned)
                    elif stride == 0:
                        turned = pltpu.roll(block, shift[0], 1)
                    else:
                        turned = pltpu.roll(block, shift[0], 1)
                        step = min(stride, 16)
                        for _ in range(stride // step):
                            turned = pltpu.roll(turned, 0, 1, stride=step, stride_axis=0)
                    for wrap in (False, True):
                        keep = (offset < wide) & (wraps == wrap)
                        moved[d].append(jnp.where(keep, turned, 0.0))
    pick = jnp.concatenate([p.astype(F32) for p in picks], axis=1).astype(BF16)
    for d in range(DETS):
        data = jnp.concatenate(moved[d], axis=0).astype(BF16)
        flat[:, d * LANES : (d + 1) * LANES] = jnp.dot(pick, data, preferred_element_type=F32)


def filter_kernel(rates_ref, seen_ref, bank_ref, out_ref, flat, hankel):
    rate = rates_ref[0]
    for r in range(5):

        @pl.when(rate == r)
        def _(r=r):
            flatten(r, seen_ref, flat)

    square = (LANES, LANES)
    later = iota(square, 1) > iota(square, 0)
    blocks = OUT0 // LANES + TAPS // LANES - 1
    for d in range(DETS):
        cols = slice(d * LANES, (d + 1) * LANES)
        turned = None
        for m in range(blocks + 1):
            line = jnp.broadcast_to(flat[m : m + 1, cols], square)
            following = pltpu.roll(line, 1, 1, stride=1, stride_axis=0)
            if m:
                hankel[(m - 1) * LANES : m * LANES, cols] = jnp.where(
                    later, following, turned
                ).astype(BF16)
            turned = following

    def power(c):
        snr = jnp.dot(
            bank_ref[...], hankel[c * LANES : c * LANES + TAPS, :], preferred_element_type=F32
        )
        each = snr[:PART] * snr[:PART] + snr[PART:] * snr[PART:]
        total = each[:, :LANES]
        for d in range(1, DETS):
            total = total + each[:, d * LANES : (d + 1) * LANES]
        return total

    @pl.when(rate == 0)
    def _():
        for c in range(OUT0 // LANES):
            out_ref[0, :, c * LANES : (c + 1) * LANES] = power(c)

    @pl.when(rate > 0)
    def _():
        total = jnp.concatenate([power(0), power(1)], axis=1)
        high = total.astype(BF16)
        rest = total - high.astype(F32)
        middle = rest.astype(BF16)
        low = (rest - middle.astype(F32)).astype(BF16)
        shape = (2 * LANES, OUT0)
        spread = (iota(shape, 1) >> rate) == iota(shape, 0)
        spread = spread.astype(F32).astype(BF16)
        out = jnp.dot(high, spread, preferred_element_type=F32)
        out = out + jnp.dot(middle, spread, preferred_element_type=F32)
        out_ref[0] = out + jnp.dot(low, spread, preferred_element_type=F32)


def on_device(strain, filters, mixing, counts, rate_bands):
    smem = pl.BlockSpec(memory_space=pltpu.SMEM)
    vmem = pl.BlockSpec(memory_space=pltpu.VMEM)
    anywhere = pl.BlockSpec(memory_space=pl.ANY)
    dma = pltpu.SemaphoreType.DMA
    seen, bank = pl.pallas_call(
        gather_kernel,
        out_shape=(
            jax.ShapeDtypeStruct((NE, NY, 16, LANES), BF16),
            jax.ShapeDtypeStruct((2 * PART, TAPS), BF16),
        ),
        in_specs=[smem, vmem, anywhere, anywhere],
        out_specs=(vmem, vmem),
        scratch_shapes=[
            pltpu.VMEM((1, 3 * LANES), F32),
            pltpu.VMEM((8 * NZ, LANES), F32),
            pltpu.VMEM((1, KMAX, TAPS), BF16),
            pltpu.VMEM((1, 2, PART, KMAX), BF16),
            dma((2,)),
            dma((NZ - 1,)),
            dma((NZ - 1,)),
            dma((NY - 1,)),
            dma((NY - 1,)),
            dma((NE - 1,)),
            dma((NE - 1,)),
        ],
        compiler_params=pltpu.CompilerParams(
            collective_id=0, has_side_effects=True, vmem_limit_bytes=24 * 2**20
        ),
        name="gather_and_mix",
    )(counts, strain, filters, mixing)
    return pl.pallas_call(
        filter_kernel,
        out_shape=jax.ShapeDtypeStruct((1, PART, OUT0), F32),
        in_specs=[smem, vmem, vmem],
        out_specs=vmem,
        scratch_shapes=[
            pltpu.VMEM((16, DETS * LANES), F32),
            pltpu.VMEM((11 * LANES, DETS * LANES), BF16),
        ],
        compiler_params=pltpu.CompilerParams(vmem_limit_bytes=24 * 2**20),
        name="filter_and_sum",
    )(rate_bands, seen, bank)


def solution(mesh):
    placed = (
        P("det", "bins"),
        P("bins", None, None),
        P("bins", None, None, None),
        P("bins"),
        P("bins"),
    )
    return jax.shard_map(
        on_device, mesh=mesh, in_specs=placed, out_specs=P("bins", "det", None), check_vma=False
    )
```

profile of v0, /device:TPU:1, one launch (start us, length us, event | category | flops | bytes accessed | tf_op | source)
XLA Modules:
  0.0 28.0 jit_solution(10508231621413543113)
XLA Ops:
  0.0 0.0 copy-start.2
  1.3 0.0 copy-done.2
  1.3 0.0 copy-start
  1.3 1.2 %copy-done = bf16[1,512,1024]{2,1,0:T(8,128)(2,1)S(1)} copy-done((bf16[1,512,1024]{2,1,0:T(8,128)(2,1)S(1)}, bf16[1,512,1024]{2,1,0:T(8,128)(2,1)}, u32[]{:S(2)}) %copy-start) | copy-done | bytes 1048600
  2.5 0.0 copy-start.1
  2.6 1.0 %copy-done.1 = bf16[1,2,256,512]{3,2,1,0:T(8,128)(2,1)S(1)} copy-done((bf16[1,2,256,512]{3,2,1,0:T(8,128)(2,1)S(1)}, bf16[1,2,256,512]{3,2,1,0:T(8,128)(2,1)}, u32[]{:S(2)}) %copy-start.1) | copy-done | bytes 524312
  3.6 22.2 %gather_and_mix.1 = (bf16[8,4,16,128]{3,2,1,0:T(8,128)(2,1)S(1)}, bf16[128,1024]{1,0:T(8,128)(2,1)S(1)}) custom-call(s32[1]{0:T(128)S(6)} %copy.6.counts_ref, f32[1,272]{1,0:T(1,128)S(1)} %copy-done.2, bf16[1,512,1024]{2,1,0:T(8,128)(2,1)S(1)} %copy-done, bf16[1,2,256,512]{3,2,1,0:T(8,128)(2,1)S(1)} %copy-done.1), custom_call_target="tpu_custom_call" | custom-call | tf_op jit(solution)/shard_map/gather_and_mix/pallas_call | solution.py:284
  25.8 2.2 %filter_and_sum.1 = f32[1,64,512]{2,1,0:T(8,128)} custom-call(s32[1]{0:T(128)S(6)} %copy.7.rates_ref, bf16[8,4,16,128]{3,2,1,0:T(8,128)(2,1)S(1)} %get-tuple-element.7.seen_ref, bf16[128,1024]{1,0:T(8,128)(2,1)S(1)} %get-tuple-element.8.bank_ref), custom_call_target="tpu_custom_call" | custom-call | tf_op jit(solution)/shard_map/filter_and_sum/pallas_call | solution.py:310
Async XLA Ops:
  0.0 1.3 %copy-start.2 = (f32[1,272]{1,0:T(1,128)S(1)}, f32[1,272]{1,0:T(1,128)}, u32[]{:S(2)}) copy-start(f32[1,272]{1,0:T(1,128)} %strain_ref.1) | copy-start | bytes 3268
  1.3 1.2 %copy-start = (bf16[1,512,1024]{2,1,0:T(8,128)(2,1)S(1)}, bf16[1,512,1024]{2,1,0:T(8,128)(2,1)}, u32[]{:S(2)}) copy-start(bf16[1,512,1024]{2,1,0:T(8,128)(2,1)} %filters_ref.1) | copy-start | bytes 3145732
  2.5 1.0 %copy-start.1 = (bf16[1,2,256,512]{3,2,1,0:T(8,128)(2,1)S(1)}, bf16[1,2,256,512]{3,2,1,0:T(8,128)(2,1)}, u32[]{:S(2)}) copy-start(bf16[1,2,256,512]{3,2,1,0:T(8,128)(2,1)} %mixing_ref.1) | copy-start | bytes 1572868
where the time goes:
time: 28.2 us; the launch traced here: 28 us
  Pallas kernels  24.4 us (87%)
  local copies, waits for them, and re-layouts  2.26 us (8%)
  between operations  1.34 us (5%)
    pallas_call x1, Pallas kernels, on_device(): pl.pallas_call(gather_kernel, out_shape=(jax.ShapeDtypeStruct((NE, NY, 16...  22.2 us
    unnamed x6, local copies, waits for them, and re-layouts  2.26 us
    pallas_call x1, Pallas kernels, on_device(): pl.pallas_call(filter_kernel, out_shape=jax.ShapeDtypeStruct((1, PART, OU...  2.19 us

commit v1 on v0

--- a/solution.py
+++ b/solution.py
@@ -13,7 +13,6 @@
 SAMPLES = 17408
 SHARD = 272
 NZ, NY, NX = 8, 4, 2
-NE = NX * DETS
 PART = TPL // DETS
 LANES = 128
 MESH = pl.DeviceIdType.MESH
@@ -38,54 +37,69 @@
     return matrix.astype(BF16)
 
 
+def hops(step, n):
+    return min(step, n - step)
+
+
 def gather_kernel(
-    counts_ref,
-    strain_ref,
-    filters_ref,
-    mixing_ref,
+    counts_hbm,
+    rates_hbm,
+    strain_hbm,
+    filters_hbm,
+    mixing_hbm,
     seen_ref,
     bank_ref,
+    rates_ref,
+    counts,
+    rates,
+    strain,
     padded,
     column,
     filters,
     mixing,
     local_sem,
-    zs,
-    zr,
-    ys,
-    yr,
-    es,
-    er,
+    line_send,
+    line_recv,
+    plane_send,
+    plane_recv,
 ):
     at_bin = lax.axis_index("bins")
     det = lax.axis_index("det")
     z = at_bin // (NY * NX)
     y = (at_bin // NX) % NY
-    xh = at_bin % NX
-    e = xh * DETS + det
-
-    def bin_of(z, y, xh):
-        return (z * NY + y) * NX + xh
-
-    z_peers = [(bin_of((z + k) % NZ, y, xh), det) for k in range(1, NZ)]
-    y_peers = [(bin_of(z, (y + k) % NY, xh), det) for k in range(1, NY)]
-    e_peers = []
-    for k in range(1, NE):
-        other = (e + k) % NE
-        e_peers.append((bin_of(z, y, other // DETS), other % DETS))
-
+    x = (at_bin % NX) * 2 + det // 2
+    core = det % 2
+
+    def device(z, y, x, core):
+        return (z * NY + y) * NX + x // 2, (x % 2) * 2 + core
+
+    line = [(dz, dc) for dz in range(NZ) for dc in range(2)][1:]
+    line.sort(key=lambda step: -hops(step[0], NZ))
+    plane = [(dy, dx) for dy in range(NY) for dx in range(4)][1:]
+    plane.sort(key=lambda step: -hops(step[0], NY) - hops(step[1], 4))
+    line_peers = [device((z + dz) % NZ, y, x, (core + dc) % 2) for dz, dc in line]
+    plane_peers = [device(z, (y + dy) % NY, (x + dx) % 4, core) for dy, dx in plane]
+
+    load_strain = pltpu.make_async_copy(strain_hbm, strain, local_sem.at[0])
+    load_strain.start()
     barrier = pltpu.get_barrier_semaphore()
-    for peer in z_peers + y_peers + e_peers:
+    for peer in line_peers + plane_peers:
         pl.semaphore_signal(barrier, inc=1, device_id=peer, device_id_type=MESH)
 
-    load_filters = pltpu.make_async_copy(filters_ref, filters, local_sem.at[0])
-    load_filters.start()
     rows = pl.ds(pl.multiple_of(det * PART, PART), PART)
-    load_mixing = pltpu.make_async_copy(mixing_ref.at[:, :, rows, :], mixing, local_sem.at[1])
-    load_mixing.start()
+    loads = [
+        pltpu.make_async_copy(counts_hbm, counts, local_sem.at[1]),
+        pltpu.make_async_copy(rates_hbm, rates, local_sem.at[2]),
+        pltpu.make_async_copy(mixing_hbm.at[:, :, rows, :], mixing, local_sem.at[3]),
+        pltpu.make_async_copy(filters_hbm, filters, local_sem.at[4]),
+    ]
+    for load in loads:
+        load.start()
 
     padded[...] = jnp.zeros_like(padded)
-    padded[:, 0:SHARD] = strain_ref[...]
+    matrix = ladder_matrix()
+    load_strain.wait()
+    padded[:, 0:SHARD] = strain[...]
     samples = padded[...]
     high = samples.astype(BF16).astype(F32)
     middle = (samples - high).astype(BF16).astype(F32)
@@ -95,18 +109,18 @@
     parts = jnp.where(
         part == 0, wide[0], jnp.where(part == 1, wide[1], jnp.where(part == 2, wide[2], 0.0))
     )
-    split = jnp.dot(parts.astype(BF16), ladder_matrix(), preferred_element_type=F32)
+    split = jnp.dot(parts.astype(BF16), matrix, preferred_element_type=F32)
     ladder = jnp.sum(split, axis=0, keepdims=True)
     row = iota((8, LANES), 0)
     tile = jnp.zeros((8, LANES), F32)
     lines = [ladder[:, :LANES], ladder[:, LANES:]]
     lines += [samples[:, k * LANES : (k + 1) * LANES] for k in range(3)]
-    for k, line in enumerate(lines):
-        tile = jnp.where(row == k, jnp.broadcast_to(line, (8, LANES)), tile)
-    own = pl.ds(pl.multiple_of(z * 8, 8), 8)
+    for k, one in enumerate(lines):
+        tile = jnp.where(row == k, jnp.broadcast_to(one, (8, LANES)), tile)
+    own = pl.ds(pl.multiple_of((core * NZ + z) * 8, 8), 8)
     column[own, :] = tile
 
-    pl.semaphore_wait(barrier, NZ + NY + NE - 3)
+    pl.semaphore_wait(barrier, len(line_peers) + len(plane_peers))
 
     def send(ref, send_sem, recv_sem, peer):
         copy = pltpu.make_async_remote_copy(
@@ -120,36 +134,44 @@
         copy.start()
         return copy
 
-    z_copies = [send(column.at[own, :], zs.at[k], zr.at[k], p) for k, p in enumerate(z_peers)]
-
-    load_mixing.wait()
-    live = iota((1, KMAX), 1) < counts_ref[0]
-    load_filters.wait()
+    line_copies = [
+        send(column.at[own, :], line_send.at[k], line_recv.at[k], peer)
+        for k, peer in enumerate(line_peers)
+    ]
+
+    for load in loads:
+        load.wait()
+    rates_ref[...] = jnp.full((8, LANES), rates[0, 0], jnp.int32)
+    live = iota((1, KMAX), 1) < counts[0, 0]
     mixed = mixing[...].reshape(2 * PART, KMAX)
     mixed = jnp.where(live, mixed, jnp.zeros_like(mixed))
-    bank = jnp.dot(mixed, filters[0], preferred_element_type=F32)
-    bank = bank.astype(BF16)
+    bank = jnp.dot(mixed, filters[0], preferred_element_type=F32).astype(BF16)
     square = (LANES, LANES)
     turn = (iota(square, 0) + iota(square, 1) == LANES - 1).astype(F32).astype(BF16)
     for a in range(TAPS // LANES):
         taps = slice(a * LANES, (a + 1) * LANES)
         bank_ref[:, taps] = jnp.dot(bank[:, taps], turn, preferred_element_type=F32).astype(BF16)
 
-    for copy in z_copies:
+    for copy in line_copies:
         copy.wait_recv()
-    low_rows = column[pl.ds(1, 8, stride=8), :]
-    last = column[8 * (NZ - 1) : 8 * NZ, :]
-    before = column[8 * (NZ - 2) : 8 * (NZ - 1), :]
-    high_rows = jnp.where(row == 5, jnp.broadcast_to(before[0:1], (8, LANES)), last)
-    seen_ref[e, y] = jnp.concatenate([low_rows, high_rows], axis=0).astype(BF16)
-
-    y_copies = [send(seen_ref.at[e, y], ys.at[k], yr.at[k], p) for k, p in enumerate(y_peers)]
-    for copy in y_copies:
+    place = y * 4 + x
+    for c in range(2):
+        first = c * NZ * 8
+        low_rows = column[pl.ds(first + 1, 8, stride=8), :]
+        last = column[first + 56 : first + 64, :]
+        before = column[first + 48 : first + 56, :]
+        high_rows = jnp.where(row == 5, jnp.broadcast_to(before[0:1], (8, LANES)), last)
+        seen_ref[place, c] = jnp.concatenate([low_rows, high_rows], axis=0).astype(BF16)
+
+    plane_copies = [
+        send(seen_ref.at[place], plane_send.at[k], plane_recv.at[k], peer)
+        for k, peer in enumerate(plane_peers)
+    ]
+    for copy in line_copies:
+        copy.wait_send()
+    for copy in plane_copies:
         copy.wait_recv()
-    e_copies = [send(seen_ref.at[e], es.at[k], er.at[k], p) for k, p in enumerate(e_peers)]
-    for copy in e_copies:
-        copy.wait_recv()
-    for copy in z_copies + y_copies + e_copies:
+    for copy in plane_copies:
         copy.wait_send()
 
 
@@ -197,7 +219,7 @@
                 for wrap in (False, True):
                     picks.append((begin_col >> 7) + int(wrap) == out_row16)
                 for d in range(DETS):
-                    block = seen_ref[xh * DETS + d, y].astype(F32)[8 * half : 8 * half + 8]
+                    block = seen_ref[y * 4 + xh * 2 + d // 2, d % 2].astype(F32)[8 * half : 8 * half + 8]
                     if stride is None:
                         turned = jnp.zeros((8, LANES), F32)
                         for amount in sorted(set(s for s, w in zip(shift, widths) if w)):
@@ -224,7 +246,7 @@
 
 
 def filter_kernel(rates_ref, seen_ref, bank_ref, out_ref, flat, hankel):
-    rate = rates_ref[0]
+    rate = rates_ref[...][0, 0]
     for r in range(5):
 
         @pl.when(rate == r)
@@ -277,40 +299,43 @@
 
 
 def on_device(strain, filters, mixing, counts, rate_bands):
-    smem = pl.BlockSpec(memory_space=pltpu.SMEM)
     vmem = pl.BlockSpec(memory_space=pltpu.VMEM)
-    anywhere = pl.BlockSpec(memory_space=pl.ANY)
+    hbm = pl.BlockSpec(memory_space=pltpu.HBM)
     dma = pltpu.SemaphoreType.DMA
-    seen, bank = pl.pallas_call(
+    given = (counts.reshape(1, 1), rate_bands.reshape(1, 1), strain, filters, mixing)
+    given = given[:2] + tuple(pltpu.with_memory_space_constraint(one, pltpu.HBM) for one in given[2:])
+    seen, bank, rates = pl.pallas_call(
         gather_kernel,
         out_shape=(
-            jax.ShapeDtypeStruct((NE, NY, 16, LANES), BF16),
+            jax.ShapeDtypeStruct((NY * 4, 2, 16, LANES), BF16),
             jax.ShapeDtypeStruct((2 * PART, TAPS), BF16),
+            jax.ShapeDtypeStruct((8, LANES), jnp.int32),
         ),
-        in_specs=[smem, vmem, anywhere, anywhere],
-        out_specs=(vmem, vmem),
+        in_specs=[hbm] * 5,
+        out_specs=(vmem, vmem, vmem),
         scratch_shapes=[
+            pltpu.SMEM((1, 1), jnp.int32),
+            pltpu.SMEM((1, 1), jnp.int32),
+            pltpu.VMEM((1, SHARD), F32),
             pltpu.VMEM((1, 3 * LANES), F32),
-            pltpu.VMEM((8 * NZ, LANES), F32),
+            pltpu.VMEM((2 * NZ * 8, LANES), F32),
             pltpu.VMEM((1, KMAX, TAPS), BF16),
             pltpu.VMEM((1, 2, PART, KMAX), BF16),
-            dma((2,)),
-            dma((NZ - 1,)),
-            dma((NZ - 1,)),
-            dma((NY - 1,)),
-            dma((NY - 1,)),
-            dma((NE - 1,)),
-            dma((NE - 1,)),
+            dma((5,)),
+            dma((2 * NZ - 1,)),
+            dma((2 * NZ - 1,)),
+            dma((NY * 4 - 1,)),
+            dma((NY * 4 - 1,)),
         ],
         compiler_params=pltpu.CompilerParams(
             collective_id=0, has_side_effects=True, vmem_limit_bytes=24 * 2**20
         ),
         name="gather_and_mix",
-    )(counts, strain, filters, mixing)
+    )(*given)
     return pl.pallas_call(
         filter_kernel,
         out_shape=jax.ShapeDtypeStruct((1, PART, OUT0), F32),
-        in_specs=[smem, vmem, vmem],
+        in_specs=[vmem, vmem, vmem],
         out_specs=vmem,
         scratch_shapes=[
             pltpu.VMEM((16, DETS * LANES), F32),
@@ -318,7 +343,7 @@
         ],
         compiler_params=pltpu.CompilerParams(vmem_limit_bytes=24 * 2**20),
         name="filter_and_sum",
-    )(rate_bands, seen, bank)
+    )(rates, seen, bank)
 
 
 def solution(mesh):

time: 28.2 us -> 23.4 us (0.83)
  Pallas kernels: 24.4 us -> 22 us
  local copies, waits for them, and re-layouts: 2.26 us -> 0 us
    pallas_call x1, Pallas kernels: 22.2 us -> 19.6 us  [on_device(): pl.pallas_call(gather_kernel, out_shape=(jax.ShapeDtypeStruct((NY * 4, 2,...]
    unnamed x6 -> x0, local copies, waits for them, and re-layouts: 2.26 us -> none
where the time goes in v1:
time: 23.4 us; the launch traced here: 23.3 us
  Pallas kernels  22 us (94%)
  between operations  1.3 us (6%)
    pallas_call x1, Pallas kernels, on_device(): pl.pallas_call(gather_kernel, out_shape=(jax.ShapeDtypeStruct((NY * 4, 2,...  19.6 us
    pallas_call x1, Pallas kernels, on_device(): pl.pallas_call(filter_kernel, out_shape=jax.ShapeDtypeStruct((1, PART, OU...  2.35 us

profile of v1, /device:TPU:1, one launch (start us, length us, event | category | flops | bytes accessed | tf_op | source)
XLA Modules:
  0.0 23.3 jit_solution(6872055110811052578)
XLA Ops:
  1.3 19.6 %gather_and_mix.1 = (bf16[16,2,16,128]{3,2,1,0:T(8,128)(2,1)S(1)}, bf16[128,1024]{1,0:T(8,128)(2,1)S(1)}, s32[8,128]{1,0:T(8,128)S(1)}) custom-call(s32[1,1]{1,0:T(1,128)} %bitcast.2.counts_hbm, s32[1,1]{1,0:T(1,128)} %bitcast.3.rates_hbm, f32[1,272]{1,0:T(1,128)} %strain_hbm.1, bf16[1,512,1024]{2,1,0:T(8,128)(2,1)} %filters_hbm.1, ...), custom_call_target="tpu_custom_call" | custom-call | tf_op jit(solution)/shard_map/gather_and_mix/pallas_call | solution.py:307
  20.9 2.3 %filter_and_sum.1 = f32[1,64,512]{2,1,0:T(8,128)} custom-call(s32[8,128]{1,0:T(8,128)S(1)} %get-tuple-element.8.rates_ref, bf16[16,2,16,128]{3,2,1,0:T(8,128)(2,1)S(1)} %get-tuple-element.9.seen_ref, bf16[128,1024]{1,0:T(8,128)(2,1)S(1)} %get-tuple-element.10.bank_ref), custom_call_target="tpu_custom_call" | custom-call | tf_op jit(solution)/shard_map/filter_and_sum/pallas_call | solution.py:335

commit v2 on v1

--- a/solution.py
+++ b/solution.py
@@ -21,6 +21,19 @@
 WIDTH = (272, 136, 68, 34, 17)
 COLUMN = (0, 0, 136, 204, 238)
 START = tuple((SAMPLES >> r) - (OUT0 >> r) - (TAPS - 1) for r in range(5))
+
+
+LINES = (
+    (4, 1, 110, 0, 17),
+    (3, 1, 76, 0, 34),
+    (2, 1, 8, 0, 68),
+    (1, 0, 0, 0, 128),
+    (1, 1, 0, 128, 8),
+    (0, 2, 0, 0, 128),
+    (0, 3, 0, 128, 128),
+    (0, 4, 0, 256, 16),
+)
+ROWS = ((5, 7), (0, 3), (2, 4), (4, 7), (0, 7))
 
 
 def iota(shape, dim):
@@ -112,11 +125,15 @@
     split = jnp.dot(parts.astype(BF16), matrix, preferred_element_type=F32)
     ladder = jnp.sum(split, axis=0, keepdims=True)
     row = iota((8, LANES), 0)
+    lane = iota((8, LANES), 1)
+    halves = [ladder[:, :LANES], ladder[:, LANES:]]
+    halves += [samples[:, k * LANES : (k + 1) * LANES] for k in range(3)]
     tile = jnp.zeros((8, LANES), F32)
-    lines = [ladder[:, :LANES], ladder[:, LANES:]]
-    lines += [samples[:, k * LANES : (k + 1) * LANES] for k in range(3)]
-    for k, one in enumerate(lines):
-        tile = jnp.where(row == k, jnp.broadcast_to(one, (8, LANES)), tile)
+    for k, (r, half, first, skip, width) in enumerate(LINES):
+        line = jnp.broadcast_to(halves[half], (8, LANES))
+        line = jnp.where((lane >= first) & (lane < first + width), line, 0.0)
+        turn = (WIDTH[r] * at_bin + skip + (LANES * 256 - START[r] - first)) % LANES
+        tile = jnp.where(row == k, pltpu.roll(line, turn, 1), tile)
     own = pl.ds(pl.multiple_of((core * NZ + z) * 8, 8), 8)
     column[own, :] = tile
 
@@ -157,11 +174,16 @@
     place = y * 4 + x
     for c in range(2):
         first = c * NZ * 8
-        low_rows = column[pl.ds(first + 1, 8, stride=8), :]
+        lines = [column[pl.ds(first + k, 8, stride=8), :] for k in range(5)]
         last = column[first + 56 : first + 64, :]
-        before = column[first + 48 : first + 56, :]
-        high_rows = jnp.where(row == 5, jnp.broadcast_to(before[0:1], (8, LANES)), last)
-        seen_ref[place, c] = jnp.concatenate([low_rows, high_rows], axis=0).astype(BF16)
+        low = lines[0] + pltpu.roll(lines[0], 5, 0)
+        low = low + jnp.where(row < 2, pltpu.roll(lines[0], 2, 0), 0.0)
+        tail = pltpu.roll(lines[4], 5, 0) + pltpu.roll(lines[4], 4, 0)
+        top = jnp.where(row < 3, low, jnp.where(row < 4, tail, lines[1]))
+        bottom = jnp.where(row < 2, pltpu.roll(lines[3], 2, 0), pltpu.roll(lines[2], 5, 0))
+        bottom = jnp.where(row < 5, bottom, last)
+        packed = jnp.concatenate([top, bottom], axis=0)
+        seen_ref[place, c] = packed.astype(BF16)
 
     plane_copies = [
         send(seen_ref.at[place], plane_send.at[k], plane_recv.at[k], peer)
@@ -175,127 +197,120 @@
         copy.wait_send()
 
 
+def begins(r, k, j):
+    at, extra = k, 0
+    if r == 2:
+        at = k + 3
+    if r == 1:
+        at, extra = (k & 1) + 6, LANES * (k >> 1)
+    if r == 0:
+        at, extra = 7, LANES * (k - 5)
+    return WIDTH[r] * (8 * at + j) + extra - START[r]
+
+
 def flatten(r, seen_ref, flat):
+    least, most = ROWS[r]
+    row = iota((8, LANES), 0)
     lane = iota((8, LANES), 1)
-    row = iota((8, LANES), 0)
-    halves = {4: "low", 3: "low", 2: "low", 1: "both", 0: "high"}[r]
-    width = WIDTH[r]
-    picks = []
     moved = [[] for _ in range(DETS)]
-    out_row16 = iota((16, 8), 0)
     for y in range(NY):
         for xh in range(NX):
-            j = y * NX + xh
-            jobs = []
-            if halves == "low":
-                first = COLUMN[r] - LANES
-                jobs.append((0, [8 * z + j for z in range(8)], 0, first, [width] * 8))
-            if halves == "both":
-                jobs.append((0, [8 * z + j for z in range(8)], LANES, 0, [8] * 8))
-                jobs.append(
-                    (1, [8 * 7 + j, 0, 0, 0, 0, 8 * 6 + j, 0, 0], 0, 0, [LANES, 0, 0, 0, 0, LANES, 0, 0])
-                )
-            if halves == "high":
-                jobs.append((1, [8 * 7 + j] * 8, None, 0, [0, 0, LANES, LANES, 16, 0, 0, 0]))
-            for half, shards, skip, first, widths in jobs:
-                begin, shift = [], []
-                for k in range(8):
-                    extra = (k - 2) * LANES if skip is None else skip
-                    at = width * shards[k] + extra - START[r]
-                    begin.append(at)
-                    shift.append((at - first) % LANES)
-                stride = (shift[1] - shift[0]) % LANES
-                if any((shift[k] - shift[0] - k * stride) % LANES for k in range(8)):
-                    stride = None
-                begin_row = jnp.zeros((8, LANES), jnp.int32)
-                begin_col = jnp.zeros((16, 8), jnp.int32)
-                wide = jnp.zeros((8, LANES), jnp.int32)
-                for k in range(8):
-                    begin_row = jnp.where(row == k, begin[k], begin_row)
-                    begin_col = jnp.where(iota((16, 8), 1) == k, begin[k], begin_col)
-                    wide = jnp.where(row == k, widths[k], wide)
-                offset = (lane - begin_row) & (LANES - 1)
-                wraps = ((begin_row & (LANES - 1)) + offset) >= LANES
-                for wrap in (False, True):
-                    picks.append((begin_col >> 7) + int(wrap) == out_row16)
-                for d in range(DETS):
-                    block = seen_ref[y * 4 + xh * 2 + d // 2, d % 2].astype(F32)[8 * half : 8 * half + 8]
-                    if stride is None:
-                        turned = jnp.zeros((8, LANES), F32)
-                        for amount in sorted(set(s for s, w in zip(shift, widths) if w)):
-                            rolled = pltpu.roll(block, amount, 1)
-                            mask = jnp.zeros((8, LANES), jnp.bool_)
-                            for k in range(8):
-                                if shift[k] == amount:
-                                    mask = mask | (row == k)
-                            turned = jnp.where(mask, rolled, turned)
-                    elif stride == 0:
-                        turned = pltpu.roll(block, shift[0], 1)
-                    else:
-                        turned = pltpu.roll(block, shift[0], 1)
-                        step = min(stride, 16)
-                        for _ in range(stride // step):
-                            turned = pltpu.roll(turned, 0, 1, stride=step, stride_axis=0)
-                    for wrap in (False, True):
-                        keep = (offset < wide) & (wraps == wrap)
-                        moved[d].append(jnp.where(keep, turned, 0.0))
-    pick = jnp.concatenate([p.astype(F32) for p in picks], axis=1).astype(BF16)
-    for d in range(DETS):
-        data = jnp.concatenate(moved[d], axis=0).astype(BF16)
-        flat[:, d * LANES : (d + 1) * LANES] = jnp.dot(pick, data, preferred_element_type=F32)
-
-
-def filter_kernel(rates_ref, seen_ref, bank_ref, out_ref, flat, hankel):
-    rate = rates_ref[...][0, 0]
-    for r in range(5):
-
-        @pl.when(rate == r)
-        def _(r=r):
-            flatten(r, seen_ref, flat)
-
+            begin = begins(r, row, y * NX + xh) & (LANES - 1)
+            after = lane >= begin
+            before = lane < begin
+            if r == 4 or r == 1:
+                inside = ((lane - begin) & (LANES - 1)) < (WIDTH[4] if r == 4 else 8)
+                if r == 1:
+                    inside = inside | (row < 2)
+                after, before = after & inside, before & inside
+            for d in range(DETS):
+                pair = seen_ref[y * 4 + xh * 2 + d // 2, d % 2].astype(F32)
+                top, bottom = pair[:8], pair[8:]
+                if r == 4:
+                    block = jnp.where(row < 6, pltpu.roll(top, 3, 0), pltpu.roll(top, 6, 0))
+                    block = jnp.where(row < 3, top, block)
+                elif r == 1:
+                    block = jnp.where(row < 2, bottom, jnp.broadcast_to(top[3:4], (8, LANES)))
+                else:
+                    block = top if r == 3 else bottom
+                moved[d].append(jnp.where(after, block, 0.0))
+                moved[d].append(jnp.where(before, block, 0.0))
+    shape = (16, 2 * 8 * NY * NX)
+    at = iota(shape, 1)
+    k = at & 7
+    where = (begins(r, k, at >> 4) >> 7) + ((at >> 3) & 1)
+    pick = (where == iota(shape, 0)) & (k >= least) & (k <= most)
+    data = jnp.concatenate([jnp.concatenate(m, axis=0) for m in moved], axis=1).astype(BF16)
+    flat[...] = jnp.dot(pick.astype(F32).astype(BF16), data, preferred_element_type=F32)
+
+
+def build_hankel(flat, hankel, blocks, first=0):
     square = (LANES, LANES)
     later = iota(square, 1) > iota(square, 0)
-    blocks = OUT0 // LANES + TAPS // LANES - 1
+
     for d in range(DETS):
         cols = slice(d * LANES, (d + 1) * LANES)
         turned = None
-        for m in range(blocks + 1):
+        for m in range(first, blocks + 1):
             line = jnp.broadcast_to(flat[m : m + 1, cols], square)
             following = pltpu.roll(line, 1, 1, stride=1, stride_axis=0)
-            if m:
+            if m > first:
                 hankel[(m - 1) * LANES : m * LANES, cols] = jnp.where(
                     later, following, turned
                 ).astype(BF16)
             turned = following
 
-    def power(c):
-        snr = jnp.dot(
-            bank_ref[...], hankel[c * LANES : c * LANES + TAPS, :], preferred_element_type=F32
-        )
+
+def filter_kernel(rates_ref, seen_ref, bank_ref, out_ref, flat, hankel):
+    rate = rates_ref[...][0, 0]
+    def total_of(snr):
         each = snr[:PART] * snr[:PART] + snr[PART:] * snr[PART:]
         total = each[:, :LANES]
         for d in range(1, DETS):
             total = total + each[:, d * LANES : (d + 1) * LANES]
         return total
 
-    @pl.when(rate == 0)
-    def _():
-        for c in range(OUT0 // LANES):
-            out_ref[0, :, c * LANES : (c + 1) * LANES] = power(c)
-
-    @pl.when(rate > 0)
-    def _():
-        total = jnp.concatenate([power(0), power(1)], axis=1)
+    def power(c):
+        taps = hankel[c * LANES : c * LANES + TAPS, :]
+        return total_of(jnp.dot(bank_ref[...], taps, preferred_element_type=F32))
+
+    def repeat(total):
         high = total.astype(BF16)
         rest = total - high.astype(F32)
         middle = rest.astype(BF16)
         low = (rest - middle.astype(F32)).astype(BF16)
-        shape = (2 * LANES, OUT0)
+        shape = (total.shape[1], OUT0)
         spread = (iota(shape, 1) >> rate) == iota(shape, 0)
         spread = spread.astype(F32).astype(BF16)
         out = jnp.dot(high, spread, preferred_element_type=F32)
         out = out + jnp.dot(middle, spread, preferred_element_type=F32)
         out_ref[0] = out + jnp.dot(low, spread, preferred_element_type=F32)
+
+    blocks = TAPS // LANES
+
+    @pl.when(rate == 0)
+    def _():
+        flatten(0, seen_ref, flat)
+        build_hankel(flat, hankel, blocks + 3)
+        for c in range(OUT0 // LANES):
+            out_ref[0, :, c * LANES : (c + 1) * LANES] = power(c)
+
+    @pl.when(rate == 1)
+    def _():
+        flatten(1, seen_ref, flat)
+        build_hankel(flat, hankel, blocks + 1)
+        repeat(jnp.concatenate([power(0), power(1)], axis=1))
+
+    for r in range(2, 5):
+
+        @pl.when(rate == r)
+        def _(r=r):
+            flatten(r, seen_ref, flat)
+
+    @pl.when(rate > 1)
+    def _():
+        build_hankel(flat, hankel, blocks)
+        repeat(power(0))
 
 
 def on_device(strain, filters, mixing, counts, rate_bands):

time: 23.4 us -> 22.7 us (0.970)
  Pallas kernels: 22 us -> 21.3 us
    pallas_call x1, Pallas kernels: 2.35 us -> 1.68 us  [on_device(): pl.pallas_call(filter_kernel, out_shape=jax.ShapeDtypeStruct((1, PART, OU...]
where the time goes in v2:
time: 22.7 us; the launch traced here: 22.6 us
  Pallas kernels  21.3 us (94%)
  between operations  1.3 us (6%)
    pallas_call x1, Pallas kernels, on_device(): pl.pallas_call(gather_kernel, out_shape=(jax.ShapeDtypeStruct((NY * 4, 2,...  19.6 us
    pallas_call x1, Pallas kernels, on_device(): pl.pallas_call(filter_kernel, out_shape=jax.ShapeDtypeStruct((1, PART, OU...  1.68 us

profile of v2, /device:TPU:1, one launch (start us, length us, event | category | flops | bytes accessed | tf_op | source)
XLA Modules:
  0.0 22.6 jit_solution(9884075481927208363)
XLA Ops:
  1.3 19.6 %gather_and_mix.1 = (bf16[16,2,16,128]{3,2,1,0:T(8,128)(2,1)S(1)}, bf16[128,1024]{1,0:T(8,128)(2,1)S(1)}, s32[8,128]{1,0:T(8,128)S(1)}) custom-call(s32[1,1]{1,0:T(1,128)} %bitcast.2.counts_hbm, s32[1,1]{1,0:T(1,128)} %bitcast.3.rates_hbm, f32[1,272]{1,0:T(1,128)} %strain_hbm.1, bf16[1,512,1024]{2,1,0:T(8,128)(2,1)} %filters_hbm.1, ...), custom_call_target="tpu_custom_call" | custom-call | tf_op jit(solution)/shard_map/gather_and_mix/pallas_call | solution.py:322
  20.9 1.7 %filter_and_sum.1 = f32[1,64,512]{2,1,0:T(8,128)} custom-call(s32[8,128]{1,0:T(8,128)S(1)} %get-tuple-element.8.rates_ref, bf16[16,2,16,128]{3,2,1,0:T(8,128)(2,1)S(1)} %get-tuple-element.9.seen_ref, bf16[128,1024]{1,0:T(8,128)(2,1)S(1)} %get-tuple-element.10.bank_ref), custom_call_target="tpu_custom_call" | custom-call | tf_op jit(solution)/shard_map/filter_and_sum/pallas_call | solution.py:350

commit v3 on v2

--- a/solution.py
+++ b/solution.py
@@ -244,24 +244,26 @@
     flat[...] = jnp.dot(pick.astype(F32).astype(BF16), data, preferred_element_type=F32)
 
 
-def build_hankel(flat, hankel, blocks, first=0):
-    square = (LANES, LANES)
-    later = iota(square, 1) > iota(square, 0)
-
+def build_hankel(flat, hankel, blocks):
+    rows = 16
+    shape = (rows, LANES)
+    groups = range(LANES // rows)
+    later = [iota(shape, 1) > iota(shape, 0) + rows * g for g in groups]
     for d in range(DETS):
         cols = slice(d * LANES, (d + 1) * LANES)
         turned = None
-        for m in range(first, blocks + 1):
-            line = jnp.broadcast_to(flat[m : m + 1, cols], square)
-            following = pltpu.roll(line, 1, 1, stride=1, stride_axis=0)
-            if m > first:
-                hankel[(m - 1) * LANES : m * LANES, cols] = jnp.where(
-                    later, following, turned
-                ).astype(BF16)
+        for m in range(blocks + 1):
+            line = jnp.broadcast_to(flat[m : m + 1, cols], shape)
+            line = pltpu.roll(line, 1, 1, stride=1, stride_axis=0).astype(BF16)
+            following = [pltpu.roll(line, rows * g, 1) if g else line for g in groups]
+            if m:
+                for g in groups:
+                    at = (m - 1) * LANES + rows * g
+                    hankel[at : at + rows, cols] = jnp.where(later[g], following[g], turned[g])
             turned = following
 
 
-def filter_kernel(rates_ref, seen_ref, bank_ref, out_ref, flat, hankel):
+def filter_kernel(rates_ref, seen_ref, bank_ref, out_hbm, flat, hankel, out, sems):
     rate = rates_ref[...][0, 0]
     def total_of(snr):
         each = snr[:PART] * snr[:PART] + snr[PART:] * snr[PART:]
@@ -269,6 +271,18 @@
         for d in range(1, DETS):
             total = total + each[:, d * LANES : (d + 1) * LANES]
         return total
+
+    def copy_of(c):
+        cols = slice(c * LANES, (c + 1) * LANES)
+        return pltpu.make_async_copy(out.at[c], out_hbm.at[0, :, cols], sems.at[c])
+
+    def write(c, value):
+        out[c] = value
+        copy_of(c).start()
+
+    def finish():
+        for c in range(OUT0 // LANES):
+            copy_of(c).wait()
 
     def power(c):
         taps = hankel[c * LANES : c * LANES + TAPS, :]
@@ -282,9 +296,12 @@
         shape = (total.shape[1], OUT0)
         spread = (iota(shape, 1) >> rate) == iota(shape, 0)
         spread = spread.astype(F32).astype(BF16)
-        out = jnp.dot(high, spread, preferred_element_type=F32)
-        out = out + jnp.dot(middle, spread, preferred_element_type=F32)
-        out_ref[0] = out + jnp.dot(low, spread, preferred_element_type=F32)
+        parts = jnp.concatenate([high, middle, low], axis=0)
+        wide = jnp.dot(parts, spread, preferred_element_type=F32)
+        wide = wide[:PART] + wide[PART : 2 * PART] + wide[2 * PART :]
+        for c in range(OUT0 // LANES):
+            write(c, wide[:, c * LANES : (c + 1) * LANES])
+        finish()
 
     blocks = TAPS // LANES
 
@@ -293,7 +310,8 @@
         flatten(0, seen_ref, flat)
         build_hankel(flat, hankel, blocks + 3)
         for c in range(OUT0 // LANES):
-            out_ref[0, :, c * LANES : (c + 1) * LANES] = power(c)
+            write(c, power(c))
+        finish()
 
     @pl.when(rate == 1)
     def _():
@@ -351,10 +369,12 @@
         filter_kernel,
         out_shape=jax.ShapeDtypeStruct((1, PART, OUT0), F32),
         in_specs=[vmem, vmem, vmem],
-        out_specs=vmem,
+        out_specs=hbm,
         scratch_shapes=[
             pltpu.VMEM((16, DETS * LANES), F32),
             pltpu.VMEM((11 * LANES, DETS * LANES), BF16),
+            pltpu.VMEM((OUT0 // LANES, PART, LANES), F32),
+            dma((OUT0 // LANES,)),
         ],
         compiler_params=pltpu.CompilerParams(vmem_limit_bytes=24 * 2**20),
         name="filter_and_sum",

time: 22.7 us -> 22.8 us (level)
  no operation moved by 1% of the time
where the time goes in v3:
time: 22.8 us; the launch traced here: 22.7 us
  Pallas kernels  21.4 us (94%)
  between operations  1.3 us (6%)
    pallas_call x1, Pallas kernels, on_device(): pl.pallas_call(gather_kernel, out_shape=(jax.ShapeDtypeStruct((NY * 4, 2,...  19.6 us
    pallas_call x1, Pallas kernels, on_device(): pl.pallas_call(filter_kernel, out_shape=jax.ShapeDtypeStruct((1, PART, OU...  1.79 us

profile of v3, /device:TPU:1, one launch (start us, length us, event | category | flops | bytes accessed | tf_op | source)
XLA Modules:
  0.0 22.7 jit_solution(16482167797235458110)
XLA Ops:
  1.3 19.6 %gather_and_mix.1 = (bf16[16,2,16,128]{3,2,1,0:T(8,128)(2,1)S(1)}, bf16[128,1024]{1,0:T(8,128)(2,1)S(1)}, s32[8,128]{1,0:T(8,128)S(1)}) custom-call(s32[1,1]{1,0:T(1,128)} %bitcast.2.counts_hbm, s32[1,1]{1,0:T(1,128)} %bitcast.3.rates_hbm, f32[1,272]{1,0:T(1,128)} %strain_hbm.1, bf16[1,512,1024]{2,1,0:T(8,128)(2,1)} %filters_hbm.1, ...), custom_call_target="tpu_custom_call" | custom-call | tf_op jit(solution)/shard_map/gather_and_mix/pallas_call | solution.py:340
  20.9 1.8 %filter_and_sum.1 = f32[1,64,512]{2,1,0:T(8,128)} custom-call(s32[8,128]{1,0:T(8,128)S(1)} %get-tuple-element.8.rates_ref, bf16[16,2,16,128]{3,2,1,0:T(8,128)(2,1)S(1)} %get-tuple-element.9.seen_ref, bf16[128,1024]{1,0:T(8,128)(2,1)S(1)} %get-tuple-element.10.bank_ref), custom_call_target="tpu_custom_call" | custom-call | tf_op jit(solution)/shard_map/filter_and_sum/pallas_call | solution.py:368

commit v4 on v3

--- a/solution.py
+++ b/solution.py
@@ -54,17 +54,42 @@
     return min(step, n - step)
 
 
+def mix(sizes_ref, mixing, filters, bank_ref):
+    counts = jnp.concatenate([sizes_ref[0:1, :] >> 3] * (KMAX // LANES), axis=1)
+    mixed = mixing[...].reshape(2 * PART, KMAX)
+    mixed = jnp.where(iota((1, KMAX), 1) < counts, mixed, jnp.zeros_like(mixed))
+    bank = jnp.dot(mixed, filters[0], preferred_element_type=F32).astype(BF16)
+    square = (LANES, LANES)
+    turn = (iota(square, 0) + iota(square, 1) == LANES - 1).astype(F32).astype(BF16)
+    for a in range(TAPS // LANES):
+        taps = slice(a * LANES, (a + 1) * LANES)
+        turned = jnp.dot(bank[:, taps], turn, preferred_element_type=F32)
+        bank_ref[: 2 * PART, taps] = turned.astype(BF16)
+    rate = (sizes_ref[...] & 7).astype(F32)
+    bank_ref[2 * PART :, :LANES] = jnp.concatenate([rate, rate], axis=0).astype(BF16)
+
+
+def mix_kernel(sizes_ref, filters_hbm, mixing_hbm, bank_ref, filters, mixing, sems):
+    rows = pl.ds(pl.multiple_of(lax.axis_index("det") * PART, PART), PART)
+    loads = [
+        pltpu.make_async_copy(mixing_hbm.at[:, :, rows, :], mixing, sems.at[0]),
+        pltpu.make_async_copy(filters_hbm, filters, sems.at[1]),
+    ]
+    for load in loads:
+        load.start()
+    for load in loads:
+        load.wait()
+    mix(sizes_ref, mixing, filters, bank_ref)
+
+
 def gather_kernel(
-    counts_hbm,
-    rates_hbm,
+    sizes_hbm,
     strain_hbm,
     filters_hbm,
     mixing_hbm,
     seen_ref,
     bank_ref,
-    rates_ref,
-    counts,
-    rates,
+    sizes_ref,
     strain,
     padded,
     column,
@@ -101,10 +126,9 @@
 
     rows = pl.ds(pl.multiple_of(det * PART, PART), PART)
     loads = [
-        pltpu.make_async_copy(counts_hbm, counts, local_sem.at[1]),
-        pltpu.make_async_copy(rates_hbm, rates, local_sem.at[2]),
-        pltpu.make_async_copy(mixing_hbm.at[:, :, rows, :], mixing, local_sem.at[3]),
-        pltpu.make_async_copy(filters_hbm, filters, local_sem.at[4]),
+        pltpu.make_async_copy(sizes_hbm, sizes_ref, local_sem.at[3]),
+        pltpu.make_async_copy(mixing_hbm.at[:, :, rows, :], mixing, local_sem.at[1]),
+        pltpu.make_async_copy(filters_hbm, filters, local_sem.at[2]),
     ]
     for load in loads:
         load.start()
@@ -158,16 +182,7 @@
 
     for load in loads:
         load.wait()
-    rates_ref[...] = jnp.full((8, LANES), rates[0, 0], jnp.int32)
-    live = iota((1, KMAX), 1) < counts[0, 0]
-    mixed = mixing[...].reshape(2 * PART, KMAX)
-    mixed = jnp.where(live, mixed, jnp.zeros_like(mixed))
-    bank = jnp.dot(mixed, filters[0], preferred_element_type=F32).astype(BF16)
-    square = (LANES, LANES)
-    turn = (iota(square, 0) + iota(square, 1) == LANES - 1).astype(F32).astype(BF16)
-    for a in range(TAPS // LANES):
-        taps = slice(a * LANES, (a + 1) * LANES)
-        bank_ref[:, taps] = jnp.dot(bank[:, taps], turn, preferred_element_type=F32).astype(BF16)
+    mix(sizes_ref, mixing, filters, bank_ref)
 
     for copy in line_copies:
         copy.wait_recv()
@@ -263,8 +278,9 @@
             turned = following
 
 
-def filter_kernel(rates_ref, seen_ref, bank_ref, out_hbm, flat, hankel, out, sems):
-    rate = rates_ref[...][0, 0]
+def filter_kernel(seen_ref, bank_ref, out_hbm, flat, hankel, out, sems):
+    rate = bank_ref[2 * PART :, :LANES].astype(F32).astype(jnp.int32)[0, 0]
+
     def total_of(snr):
         each = snr[:PART] * snr[:PART] + snr[PART:] * snr[PART:]
         total = each[:, :LANES]
@@ -286,7 +302,7 @@
 
     def power(c):
         taps = hankel[c * LANES : c * LANES + TAPS, :]
-        return total_of(jnp.dot(bank_ref[...], taps, preferred_element_type=F32))
+        return total_of(jnp.dot(bank_ref[: 2 * PART], taps, preferred_element_type=F32))
 
     def repeat(total):
         high = total.astype(BF16)
@@ -335,26 +351,39 @@
     vmem = pl.BlockSpec(memory_space=pltpu.VMEM)
     hbm = pl.BlockSpec(memory_space=pltpu.HBM)
     dma = pltpu.SemaphoreType.DMA
-    given = (counts.reshape(1, 1), rate_bands.reshape(1, 1), strain, filters, mixing)
-    given = given[:2] + tuple(pltpu.with_memory_space_constraint(one, pltpu.HBM) for one in given[2:])
-    seen, bank, rates = pl.pallas_call(
+    given = (strain, filters, mixing)
+    given = [pltpu.with_memory_space_constraint(one, pltpu.HBM) for one in given]
+    params = pltpu.CompilerParams(vmem_limit_bytes=24 * 2**20)
+    bank_shape = jax.ShapeDtypeStruct((2 * PART + 16, TAPS), BF16)
+    bank_scratch = [pltpu.VMEM((1, KMAX, TAPS), BF16), pltpu.VMEM((1, 2, PART, KMAX), BF16)]
+
+    at_bin = lax.axis_index("bins")
+    place = 2 * jnp.minimum(at_bin >> 3, 4) + ((at_bin >> 1) & 3)
+    place = place + 2 * (at_bin & 1) + (lax.axis_index("det") >> 1)
+    early = place < 10
+
+    def sizes_of(counts, rates):
+        return jnp.broadcast_to(counts[0] * 8 + rates[0], (8, LANES))
+
+    def nothing(counts, rates):
+        return jnp.zeros((8, LANES), jnp.int32)
+
+    sizes = lax.cond(early, sizes_of, nothing, counts, rate_bands)
+    seen, bank = pl.pallas_call(
         gather_kernel,
         out_shape=(
             jax.ShapeDtypeStruct((NY * 4, 2, 16, LANES), BF16),
-            jax.ShapeDtypeStruct((2 * PART, TAPS), BF16),
-            jax.ShapeDtypeStruct((8, LANES), jnp.int32),
+            bank_shape,
         ),
-        in_specs=[hbm] * 5,
-        out_specs=(vmem, vmem, vmem),
+        in_specs=[hbm] * 4,
+        out_specs=(vmem, vmem),
         scratch_shapes=[
-            pltpu.SMEM((1, 1), jnp.int32),
-            pltpu.SMEM((1, 1), jnp.int32),
+            pltpu.VMEM((8, LANES), jnp.int32),
             pltpu.VMEM((1, SHARD), F32),
             pltpu.VMEM((1, 3 * LANES), F32),
             pltpu.VMEM((2 * NZ * 8, LANES), F32),
-            pltpu.VMEM((1, KMAX, TAPS), BF16),
-            pltpu.VMEM((1, 2, PART, KMAX), BF16),
-            dma((5,)),
+            *bank_scratch,
+            dma((4,)),
             dma((2 * NZ - 1,)),
             dma((2 * NZ - 1,)),
             dma((NY * 4 - 1,)),
@@ -364,11 +393,27 @@
             collective_id=0, has_side_effects=True, vmem_limit_bytes=24 * 2**20
         ),
         name="gather_and_mix",
-    )(*given)
+    )(sizes, *given)
+
+    def ready(bank, counts, rates, filters, mixing):
+        return bank
+
+    def late(bank, counts, rates, filters, mixing):
+        return pl.pallas_call(
+            mix_kernel,
+            out_shape=bank_shape,
+            in_specs=[vmem, hbm, hbm],
+            out_specs=vmem,
+            scratch_shapes=[*bank_scratch, dma((2,))],
+            compiler_params=params,
+            name="mix_late",
+        )(sizes_of(counts, rates), filters, mixing)
+
+    bank = lax.cond(early, ready, late, bank, counts, rate_bands, filters, mixing)
     return pl.pallas_call(
         filter_kernel,
         out_shape=jax.ShapeDtypeStruct((1, PART, OUT0), F32),
-        in_specs=[vmem, vmem, vmem],
+        in_specs=[vmem] * 2,
         out_specs=hbm,
         scratch_shapes=[
             pltpu.VMEM((16, DETS * LANES), F32),
@@ -376,9 +421,9 @@
             pltpu.VMEM((OUT0 // LANES, PART, LANES), F32),
             dma((OUT0 // LANES,)),
         ],
-        compiler_params=pltpu.CompilerParams(vmem_limit_bytes=24 * 2**20),
+        compiler_params=params,
         name="filter_and_sum",
-    )(rates, seen, bank)
+    )(seen, bank)
 
 
 def solution(mesh):

time: 22.8 us -> 21.9 us (0.961)
  loops' own time: 0 us -> 1.4 us
  between operations: 1.3 us -> 0.05 us
  Pallas kernels: 21.4 us -> 20.3 us
    another operation x0 -> x2, loops' own time: none -> 1.4 us  [the longest x1 1.39 us: on_device(): sizes = lax.cond(early, sizes_of, nothing, counts, rate_bands)]
    pallas_call x1, Pallas kernels: 19.6 us -> 18.5 us  [on_device(): pl.pallas_call(gather_kernel, out_shape=(jax.ShapeDtypeStruct((NY * 4, 2,...]
where the time goes in v4:
time: 21.9 us; the launch traced here: 21.8 us
  Pallas kernels  20.3 us (93%)
  loops' own time  1.4 us (6%)
    pallas_call x1, Pallas kernels, on_device(): pl.pallas_call(gather_kernel, out_shape=(jax.ShapeDtypeStruct((NY * 4, 2,...  18.5 us
    pallas_call x1, Pallas kernels, on_device(): pl.pallas_call(filter_kernel, out_shape=jax.ShapeDtypeStruct((1, PART, OU...  1.79 us
    another operation x1, loops' own time, on_device(): sizes = lax.cond(early, sizes_of, nothing, counts, rate_bands)  1.39 us

profile of v4, /device:TPU:1, one launch (start us, length us, event | category | flops | bytes accessed | tf_op | source)
XLA Modules:
  0.0 21.8 jit_solution(7460331714517166080)
XLA Ops:
  0.0 0.0 copy-start
  0.0 1.4 %conditional.2 = (s32[8,128]{1,0:T(8,128)S(1)}) conditional(s32[]{:T(128)} %convert_element_type.4, () %tuple.17, (s32[1]{0:T(128)}, s32[1]{0:T(128)}) %tuple.18), branch_computations={%region_0.0_spmd, %region_1.0_spmd} | conditional | flops 2 | bytes 4132 | solution.py:371
  1.4 0.0 copy-start.1
  1.4 18.5 %gather_and_mix.1 = (bf16[16,2,16,128]{3,2,1,0:T(8,128)(2,1)S(1)}, bf16[144,1024]{1,0:T(8,128)(2,1)S(1)}) custom-call(s32[8,128]{1,0:T(8,128)S(1)} %get-tuple-element.34.sizes_hbm, f32[1,272]{1,0:T(1,128)} %strain_hbm.1, bf16[1,512,1024]{2,1,0:T(8,128)(2,1)} %filters_hbm.1, bf16[1,2,256,512]{3,2,1,0:T(8,128)(2,1)} %mixing_hbm.1), custom_call_target="tpu_custom_call" | custom-call | tf_op jit(solution)/shard_map/gather_and_mix/pallas_call | solution.py:372
  19.9 0.0 copy-done
  20.0 0.0 copy-done.1
  20.0 1.8 %filter_and_sum.1 = f32[1,64,512]{2,1,0:T(8,128)} custom-call(bf16[16,2,16,128]{3,2,1,0:T(8,128)(2,1)S(1)} %get-tuple-element.32.seen_ref, bf16[144,1024]{1,0:T(8,128)(2,1)S(1)} %get-tuple-element.35.bank_ref), custom_call_target="tpu_custom_call" | custom-call | tf_op jit(solution)/shard_map/filter_and_sum/pallas_call | solution.py:413
  (2 shorter events, 0.0 us)
Async XLA Ops:
  0.0 19.9 %copy-start = (bf16[1,512,1024]{2,1,0:T(8,128)(2,1)S(1)}, bf16[1,512,1024]{2,1,0:T(8,128)(2,1)}, u32[]{:S(2)}) copy-start(bf16[1,512,1024]{2,1,0:T(8,128)(2,1)} %filters_hbm.1) | copy-start | bytes 3145732
  1.4 18.6 %copy-start.1 = (bf16[1,2,256,512]{3,2,1,0:T(8,128)(2,1)S(1)}, bf16[1,2,256,512]{3,2,1,0:T(8,128)(2,1)}, u32[]{:S(2)}) copy-start(bf16[1,2,256,512]{3,2,1,0:T(8,128)(2,1)} %mixing_hbm.1) | copy-start | bytes 1572868

commit v5 on v4

--- a/solution.py
+++ b/solution.py
@@ -360,7 +360,7 @@
     at_bin = lax.axis_index("bins")
     place = 2 * jnp.minimum(at_bin >> 3, 4) + ((at_bin >> 1) & 3)
     place = place + 2 * (at_bin & 1) + (lax.axis_index("det") >> 1)
-    early = place < 10
+    early = place < 9
 
     def sizes_of(counts, rates):
         return jnp.broadcast_to(counts[0] * 8 + rates[0], (8, LANES))

time: 21.9 us -> 21.6 us (0.986)
  Pallas kernels: 20.3 us -> 20 us
    pallas_call x1, Pallas kernels: 18.5 us -> 18.2 us  [on_device(): pl.pallas_call(gather_kernel, out_shape=(jax.ShapeDtypeStruct((NY * 4, 2,...]
where the time goes in v5:
time: 21.6 us; the launch traced here: 21.5 us
  Pallas kernels  20 us (93%)
  loops' own time  1.4 us (6%)
    pallas_call x1, Pallas kernels, on_device(): pl.pallas_call(gather_kernel, out_shape=(jax.ShapeDtypeStruct((NY * 4, 2,...  18.2 us
    pallas_call x1, Pallas kernels, on_device(): pl.pallas_call(filter_kernel, out_shape=jax.ShapeDtypeStruct((1, PART, OU...  1.79 us
    another operation x1, loops' own time, on_device(): sizes = lax.cond(early, sizes_of, nothing, counts, rate_bands)  1.39 us

profile of v5, /device:TPU:1, one launch (start us, length us, event | category | flops | bytes accessed | tf_op | source)
XLA Modules:
  0.0 21.5 jit_solution(382451065707830501)
XLA Ops:
  0.0 0.0 copy-start
  0.0 1.4 %conditional.2 = (s32[8,128]{1,0:T(8,128)S(1)}) conditional(s32[]{:T(128)} %convert_element_type.4, () %tuple.17, (s32[1]{0:T(128)}, s32[1]{0:T(128)}) %tuple.18), branch_computations={%region_0.0_spmd, %region_1.0_spmd} | conditional | flops 2 | bytes 4132 | solution.py:371
  1.4 0.0 copy-start.1
  1.4 18.2 %gather_and_mix.1 = (bf16[16,2,16,128]{3,2,1,0:T(8,128)(2,1)S(1)}, bf16[144,1024]{1,0:T(8,128)(2,1)S(1)}) custom-call(s32[8,128]{1,0:T(8,128)S(1)} %get-tuple-element.34.sizes_hbm, f32[1,272]{1,0:T(1,128)} %strain_hbm.1, bf16[1,512,1024]{2,1,0:T(8,128)(2,1)} %filters_hbm.1, bf16[1,2,256,512]{3,2,1,0:T(8,128)(2,1)} %mixing_hbm.1), custom_call_target="tpu_custom_call" | custom-call | tf_op jit(solution)/shard_map/gather_and_mix/pallas_call | solution.py:372
  19.6 0.0 copy-done
  19.7 0.0 copy-done.1
  19.7 1.8 %filter_and_sum.1 = f32[1,64,512]{2,1,0:T(8,128)} custom-call(bf16[16,2,16,128]{3,2,1,0:T(8,128)(2,1)S(1)} %get-tuple-element.32.seen_ref, bf16[144,1024]{1,0:T(8,128)(2,1)S(1)} %get-tuple-element.35.bank_ref), custom_call_target="tpu_custom_call" | custom-call | tf_op jit(solution)/shard_map/filter_and_sum/pallas_call | solution.py:413
  (2 shorter events, 0.0 us)
Async XLA Ops:
  0.0 19.6 %copy-start = (bf16[1,512,1024]{2,1,0:T(8,128)(2,1)S(1)}, bf16[1,512,1024]{2,1,0:T(8,128)(2,1)}, u32[]{:S(2)}) copy-start(bf16[1,512,1024]{2,1,0:T(8,128)(2,1)} %filters_hbm.1) | copy-start | bytes 3145732
  1.4 18.3 %copy-start.1 = (bf16[1,2,256,512]{3,2,1,0:T(8,128)(2,1)S(1)}, bf16[1,2,256,512]{3,2,1,0:T(8,128)(2,1)}, u32[]{:S(2)}) copy-start(bf16[1,2,256,512]{3,2,1,0:T(8,128)(2,1)} %mixing_hbm.1) | copy-start | bytes 1572868
